TPU v7x, 32 devices: a whole 2x2x4 slice. The times are simulated.
32 devices in a mesh: sub: 8 (over z, y), col: 4 (over x, core).
Axes of the slice: x: 2, y: 2, z: 4, core: 2. Of those that a mesh axis runs over, the one named last changes fastest.
Arguments:
- rhs: bfloat16 [32, 1024, 128], P(('sub', 'col')), may hold values from -64 to 64
- schur: bfloat16 [32, 1024, 1024], P(('sub', 'col')), may hold values from -1 to 3
- local_inverse: bfloat16 [32, 1024, 1024], P(('sub', 'col')), may hold values from -1 to 2
- basis: bfloat16 [32, 8, 1024], P(('sub', 'col')), may hold values from -0.75 to 0.75
- coarse_inverse: bfloat16 [256, 256], P('sub', 'col'), may hold values from -1 to 2
- primal_index: int32 [32, 8], P(('sub', 'col')), may hold values from 0 to 255, as said below
- neighbour_dof: int32 [32, 1024], P(('sub', 'col')), may hold values from 0 to 1023, as said below
Outputs:
- solution: bfloat16 [32, 1024, 128], P(('sub', 'col'))
Inputs may be any that keep to these rules, and one draw needn't show every extreme that they name: `neighbour_dof`: each subdomain's unknowns in one shared block name places in the neighbour's facing block (for [0, 256) the neighbour's [256, 512), and so on), and the neighbour's entry names the place back. `primal_index`: every coarse unknown is named exactly once over all subdomains.
All inputs are finite; a program needn't handle non-finite values.
Results may differ from a plain program's by a relative error of at most 0.004.
The roundings to bfloat16 on the way count: a program that leaves them out, or rounds other values in their place, can miss the bound.
Values may be sent and summed in bfloat16 or wider, within the bound.
A program may use at most 64 MiB of HBM per device.

v0:
```python
import jax
import jax.numpy as jnp
from jax import lax
from jax.sharding import PartitionSpec as P


def from_behind(value, axis, steps):
    count = lax.axis_size(axis)
    pairs = [(source, (source + steps) % count) for source in range(count)]
    return lax.ppermute(value, axis, pairs)


def on_device(rhs, schur, local_inverse, basis, coarse_inverse, primal_index, neighbour_dof):
    link_table = neighbour_dof[0]
    face_size = link_table.shape[0] // 4
    cases = rhs.shape[2]
    offsets = (face_size, 0, 3 * face_size, 2 * face_size)
    places = []
    for number in range(4):
        places.append(link_table[number * face_size : (number + 1) * face_size] - offsets[number])
    schur_own = schur[0]
    inverse_own = local_inverse[0]
    basis_own = basis[0]
    index_own = primal_index[0]
    column_width = coarse_inverse.shape[1]
    column_base = lax.axis_index("col") * column_width

    def combine(field, incoming):
        collected = [
            jnp.take(incoming[number].astype(jnp.float32), places[number], axis=0)
            for number in range(4)
        ]
        return field + jnp.concatenate(collected, axis=0)

    def assemble(field):
        from_below = from_behind(field[face_size : 2 * face_size], "sub", 1)
        from_above = from_behind(field[:face_size], "sub", -1)
        from_left = from_behind(field[3 * face_size :].astype(jnp.bfloat16), "col", 1).astype(
            jnp.float32
        )
        from_right = from_behind(field[2 * face_size : 3 * face_size], "col", -1)
        return combine(field, (from_below, from_above, from_left, from_right))

    def inner(left_field, right_field):
        return lax.psum(0.5 * jnp.sum(left_field * right_field, axis=0), ("sub", "col"))

    residual = assemble(rhs[0].astype(jnp.float32))
    weighted = (residual * 0.5).astype(jnp.bfloat16)
    local_part = jnp.dot(inverse_own, weighted, preferred_element_type=jnp.float32)
    coarse_load = jnp.dot(basis_own, weighted, preferred_element_type=jnp.float32).astype(
        jnp.bfloat16
    )
    start_block = jnp.zeros((column_width, cases), jnp.bfloat16)
    values = lax.all_gather(coarse_load, ("sub", "col"), axis=0, tiled=True)
    indices = lax.all_gather(index_own, ("sub", "col"), axis=0, tiled=True)
    spots = indices - column_base
    spots = jnp.where((spots >= 0) & (spots < column_width), spots, column_width)
    column_part = start_block.at[spots].set(values, mode="drop")
    partial_rows = jnp.dot(coarse_inverse, column_part, preferred_element_type=jnp.float32)
    start_taken = jnp.zeros((index_own.shape[0], cases), jnp.bfloat16)
    block_rows = lax.psum(partial_rows, "col").astype(jnp.bfloat16)
    piece = lax.all_gather(block_rows, "sub", axis=0, tiled=True)
    spots = index_own
    count = piece.shape[0]
    valid = (spots >= 0) & (spots < count)
    rows = jnp.take(piece, jnp.clip(spots, 0, count - 1), axis=0)
    taken = jnp.where(valid[:, None], rows, start_taken)
    correction = lax.dot_general(
        basis_own, taken, (((0,), (0,)), ((), ())), preferred_element_type=jnp.float32
    )
    first = assemble((local_part + correction) * 0.5)
    rz_first = inner(residual, first)
    image = assemble(
        jnp.dot(schur_own, first.astype(jnp.bfloat16), preferred_element_type=jnp.float32)
    )
    alpha = rz_first / inner(first, image)
    return (alpha * first).astype(jnp.bfloat16)[None]


def solution(mesh):
    return jax.shard_map(
        on_device,
        mesh=mesh,
        in_specs=(
            P(("sub", "col"), None, None),
            P(("sub", "col"), None, None),
            P(("sub", "col"), None, None),
            P(("sub", "col"), None, None),
            P("sub", "col"),
            P(("sub", "col"), None),
            P(("sub", "col"), None),
        ),
        out_specs=P(("sub", "col"), None, None),
        check_vma=False,
    )
```

profile of v0, /device:TPU:0, one launch (start us, length us, event | category | flops | bytes accessed | tf_op | source)
XLA Modules:
  0.0 225.9 jit_solution(8289083633915082191)
XLA Ops:
  0.0 1.2 copy.8
  1.3 3.1 %collective-permute-start = (f32[256,128]{0,1:T(8,128)S(1)}, f32[256,128]{0,1:T(8,128)S(1)}, u32[]{:S(2)}, u32[]{:S(2)}) collective-permute-start(f32[256,128]{0,1:T(8,128)S(1)} %get-tuple-element.16), channel_id=1, source_target_pairs={{0,4},{4,8},{8,12},{12,16},{16,20},{20,24},{24,28},{28,0},{1,5},{5... | collective-permute-start | bytes 393224 | tf_op jit(solution)/shard_map/ppermute | solution.py:10
  4.4 3.1 %collective-permute-start.1 = (f32[256,128]{0,1:T(8,128)S(1)}, f32[256,128]{0,1:T(8,128)S(1)}, u32[]{:S(2)}, u32[]{:S(2)}) collective-permute-start(f32[256,128]{0,1:T(8,128)S(1)} %get-tuple-element.17), channel_id=1, source_target_pairs={{0,28},{4,0},{8,4},{12,8},{16,12},{20,16},{24,20},{28,24},{1,29},{... | collective-permute-start | bytes 393224 | tf_op jit(solution)/shard_map/ppermute | solution.py:10
  12.6 37.7 %all-reduce = s32[256]{0:T(256)S(1)} all-reduce(s32[256]{0:T(256)S(1)} %bitcast_dynamic-update-slice_fusion), channel_id=2, replica_groups=mesh['sub'=8,'col'=4] {'sub','col'}, use_global_device_ids=true, to_apply=%add | all-reduce | flops 256 | bytes 2048
  52.9 1.2 broadcast_select_fusion.9
  57.4 41.2 %all_gather.10 = bf16[256,128]{1,0:T(8,128)(2,1)S(1)} all-gather(bf16[8,128]{1,0:T(8,128)(2,1)S(1)} %fusion.9), channel_id=1, replica_groups=mesh['sub'=8,'col'=4] {'sub','col'}, dimensions={0}, use_global_device_ids=true | all-gather | bytes 67584 | tf_op jit(solution)/shard_map/all_gather | solution.py:54
  98.6 1.3 scatter_custom_fusion
  100.0 10.3 %psum.21 = bf16[32,128]{1,0:T(8,128)(2,1)S(1)} all-reduce(f32[32,128]{1,0:T(8,128)S(1)} %convolution_bitcast_fusion), channel_id=1, replica_groups=mesh['sub'=8,'col'=4] {'col'}, use_global_device_ids=true, to_apply=%region_1.3 | all-reduce | flops 4096 | bytes 24576 | tf_op jit(solution)/shard_map/psum | solution.py:61
  110.4 30.5 %all_gather.11 = bf16[256,128]{1,0:T(8,128)(2,1)S(1)} all-gather(bf16[32,128]{1,0:T(8,128)(2,1)S(1)} %psum.21), channel_id=1, replica_groups=mesh['sub'=8,'col'=4] {'sub'}, dimensions={0}, use_global_device_ids=true | all-gather | bytes 73728 | tf_op jit(solution)/shard_map/all_gather | solution.py:62
  140.9 1.6 fusion.2
  143.2 1.4 fusion.8
  146.7 4.7 %collective-permute-start.5 = (f32[256,128]{0,1:T(8,128)}, f32[256,128]{0,1:T(8,128)S(1)}, u32[]{:S(2)}, u32[]{:S(2)}) collective-permute-start(f32[256,128]{0,1:T(8,128)} %get-tuple-element.15), channel_id=1, source_target_pairs={{0,28},{4,0},{8,4},{12,8},{16,12},{20,16},{24,20},{28,24},{1,29},{... | collective-permute-start | bytes 393224 | tf_op jit(solution)/shard_map/ppermute | solution.py:10
  151.9 1.3 broadcast_select_fusion.8
  153.3 2.2 collective-permute-done.6
  158.3 1.0 copy.22
  163.4 2.0 collective-permute-start.9
  165.5 1.4 collective-permute-start.11
  167.8 1.3 gather_fusion.11
  169.2 1.0 copy.29
  170.2 1.2 broadcast_select_fusion.1
  171.4 1.0 copy.26
  172.4 1.4 gather_fusion.10
  173.8 1.0 copy.27
  174.8 1.3 broadcast_select_fusion.2
  176.1 1.0 copy.24
  177.1 1.3 gather_fusion.9
  178.5 1.0 copy.25
  180.1 1.0 copy.30
  181.1 1.3 gather_fusion.12
  182.5 1.0 copy.31
  183.5 1.5 fusion.15
  185.0 39.9 %all-reduce.1 = (f32[128]{0:T(128)S(1)}, f32[128]{0:T(128)S(1)}) all-reduce(f32[128]{0:T(128)S(1)} %broadcast_multiply_fusion.1, f32[128]{0:T(128)S(1)} %broadcast_multiply_fusion), channel_id=1, replica_groups=mesh['sub'=8,'col'=4] {'sub','col'}, use_global_device_ids=true, to_apply=%region_3.5 | all-reduce | flops 256 | bytes 2048 | tf_op jit(solution)/shard_map/psum | solution.py:45
  (116 shorter events, 23.7 us)
Async XLA Ops:
  0.0 140.9 %copy-start = (bf16[1,1024,1024]{2,1,0:T(8,128)(2,1)S(1)}, bf16[1,1024,1024]{2,1,0:T(8,128)(2,1)}, u32[]{:S(2)}) copy-start(bf16[1,1024,1024]{2,1,0:T(8,128)(2,1)} %param.11) | copy-start | bytes 6291460
  0.0 9.0 %copy-start.9 = (s32[1,1024]{1,0:T(1,128)S(1)}, s32[1,1024]{1,0:T(1,128)}, u32[]{:S(2)}) copy-start(s32[1,1024]{1,0:T(1,128)} %param.15) | copy-start | bytes 12292
  0.0 11.2 %copy-start.12 = (s32[1,8]{1,0:T(1,128)S(1)}, s32[1,8]{1,0:T(1,128)}, u32[]{:S(2)}) copy-start(s32[1,8]{1,0:T(1,128)} %param.14) | copy-start | bytes 100
  1.3 52.8 %collective-permute-start = (f32[256,128]{0,1:T(8,128)S(1)}, f32[256,128]{0,1:T(8,128)S(1)}, u32[]{:S(2)}, u32[]{:S(2)}) collective-permute-start(f32[256,128]{0,1:T(8,128)S(1)} %get-tuple-element.16), channel_id=1, source_target_pairs={{0,4},{4,8},{8,12},{12,16},{16,20},{20,24},{24,28},{28,0},{1,5},{5... | collective-permute-start | bytes 393224 | tf_op jit(solution)/shard_map/ppermute | solution.py:10
  4.4 50.7 %collective-permute-start.1 = (f32[256,128]{0,1:T(8,128)S(1)}, f32[256,128]{0,1:T(8,128)S(1)}, u32[]{:S(2)}, u32[]{:S(2)}) collective-permute-start(f32[256,128]{0,1:T(8,128)S(1)} %get-tuple-element.17), channel_id=1, source_target_pairs={{0,28},{4,0},{8,4},{12,8},{16,12},{20,16},{24,20},{28,24},{1,29},{... | collective-permute-start | bytes 393224 | tf_op jit(solution)/shard_map/ppermute | solution.py:10
  7.5 48.6 %collective-permute-start.3 = (f32[256,128]{0,1:T(8,128)S(1)}, f32[256,128]{0,1:T(8,128)S(1)}, u32[]{:S(2)}, u32[]{:S(2)}) collective-permute-start(f32[256,128]{0,1:T(8,128)S(1)} %get-tuple-element.18), channel_id=1, source_target_pairs={{0,3},{1,0},{2,1},{3,2},{4,7},{5,4},{6,5},{7,6},{8,11},{9,8},{10,9... | collective-permute-start | bytes 393224 | tf_op jit(solution)/shard_map/ppermute | solution.py:10
  9.0 42.5 %collective-permute-start.2 = (bf16[256,128]{1,0:T(8,128)(2,1)S(1)}, bf16[256,128]{1,0:T(8,128)(2,1)S(1)}, u32[]{:S(2)}, u32[]{:S(2)}) collective-permute-start(bf16[256,128]{1,0:T(8,128)(2,1)S(1)} %slice_bitcast_fusion.3), channel_id=1, source_target_pairs={{0,1},{1,2},{2,3},{3,0},{4,5},{5,6},{6,7},{7,4},{8,9},{9,10},{10,1... | collective-permute-start | bytes 196616 | tf_op jit(solution)/shard_map/ppermute | solution.py:10
  55.0 2.0 copy-start.6
  55.0 2.1 copy-start.8
  55.0 2.1 copy-start.4
  56.0 1.3 copy-start.2
  56.0 43.9 %copy-start.3 = (bf16[32,64]{1,0:T(8,128)(2,1)S(1)}, bf16[32,64]{1,0:T(8,128)(2,1)}, u32[]{:S(2)}) copy-start(bf16[32,64]{1,0:T(8,128)(2,1)} %param.13) | copy-start | bytes 12292
  57.1 86.1 %copy-start.10 = (pred[8]{0:T(512)(128)(4,1)S(1)}, pred[8]{0:T(512)(128)(4,1)}, u32[]{:S(2)}) copy-start(pred[8]{0:T(512)(128)(4,1)} %and_bitcast_fusion) | copy-start | bytes 28
  57.1 86.1 %copy-start.11 = (pred[8]{0:T(512)(128)(4,1)S(1)}, pred[8]{0:T(512)(128)(4,1)}, u32[]{:S(2)}) copy-start(pred[8]{0:T(512)(128)(4,1)} %compare_and_fusion.4) | copy-start | bytes 28
  146.7 9.7 %collective-permute-start.4 = (f32[256,128]{0,1:T(8,128)}, f32[256,128]{0,1:T(8,128)S(1)}, u32[]{:S(2)}, u32[]{:S(2)}) collective-permute-start(f32[256,128]{0,1:T(8,128)} %get-tuple-element.13), channel_id=1, source_target_pairs={{0,4},{4,8},{8,12},{12,16},{16,20},{20,24},{24,28},{28,0},{1,5},{5... | collective-permute-start | bytes 393224 | tf_op jit(solution)/shard_map/ppermute | solution.py:10
  146.7 10.6 %collective-permute-start.5 = (f32[256,128]{0,1:T(8,128)}, f32[256,128]{0,1:T(8,128)S(1)}, u32[]{:S(2)}, u32[]{:S(2)}) collective-permute-start(f32[256,128]{0,1:T(8,128)} %get-tuple-element.15), channel_id=1, source_target_pairs={{0,28},{4,0},{8,4},{12,8},{16,12},{20,16},{24,20},{28,24},{1,29},{... | collective-permute-start | bytes 393224 | tf_op jit(solution)/shard_map/ppermute | solution.py:10
  151.4 6.8 %collective-permute-start.7 = (f32[256,128]{0,1:T(8,128)}, f32[256,128]{0,1:T(8,128)}, u32[]{:S(2)}, u32[]{:S(2)}) collective-permute-start(f32[256,128]{0,1:T(8,128)} %get-tuple-element.14), channel_id=1, source_target_pairs={{0,3},{1,0},{2,1},{3,2},{4,7},{5,4},{6,5},{7,6},{8,11},{9,8},{10,9... | collective-permute-start | bytes 393224 | tf_op jit(solution)/shard_map/ppermute | solution.py:10
  151.4 4.0 %collective-permute-start.6 = (bf16[256,128]{0,1:T(8,128)(2,1)S(1)}, bf16[256,128]{0,1:T(8,128)(2,1)S(1)}, u32[]{:S(2)}, u32[]{:S(2)}) collective-permute-start(bf16[256,128]{0,1:T(8,128)(2,1)S(1)} %slice.134), channel_id=1, source_target_pairs={{0,1},{1,2},{2,3},{3,0},{4,5},{5,6},{6,7},{7,4},{8,9},{9,10},{10,1... | collective-permute-start | bytes 196616 | tf_op jit(solution)/shard_map/ppermute | solution.py:10
  160.1 1.6 copy-start.1
  162.6 4.3 %collective-permute-start.10 = (bf16[256,128]{0,1:T(8,128)(2,1)S(1)}, bf16[256,128]{0,1:T(8,128)(2,1)}, u32[]{:S(2)}, u32[]{:S(2)}) collective-permute-start(bf16[256,128]{0,1:T(8,128)(2,1)S(1)} %slice.133), channel_id=1, source_target_pairs={{0,1},{1,2},{2,3},{3,0},{4,5},{5,6},{6,7},{7,4},{8,9},{9,10},{10,1... | collective-permute-start | bytes 196616 | tf_op jit(solution)/shard_map/ppermute | solution.py:10
  163.4 8.0 %collective-permute-start.9 = (f32[256,128]{0,1:T(8,128)}, f32[256,128]{0,1:T(8,128)}, u32[]{:S(2)}, u32[]{:S(2)}) collective-permute-start(f32[256,128]{0,1:T(8,128)} %get-tuple-element.12), channel_id=1, source_target_pairs={{0,28},{4,0},{8,4},{12,8},{16,12},{20,16},{24,20},{28,24},{1,29},{... | collective-permute-start | bytes 393224 | tf_op jit(solution)/shard_map/ppermute | solution.py:10
  165.4 10.7 %collective-permute-start.8 = (f32[256,128]{0,1:T(8,128)}, f32[256,128]{0,1:T(8,128)}, u32[]{:S(2)}, u32[]{:S(2)}) collective-permute-start(f32[256,128]{0,1:T(8,128)} %get-tuple-element.10), channel_id=1, source_target_pairs={{0,4},{4,8},{8,12},{12,16},{16,20},{20,24},{24,28},{28,0},{1,5},{5... | collective-permute-start | bytes 393224 | tf_op jit(solution)/shard_map/ppermute | solution.py:10
  165.5 14.7 %collective-permute-start.11 = (f32[256,128]{0,1:T(8,128)}, f32[256,128]{0,1:T(8,128)}, u32[]{:S(2)}, u32[]{:S(2)}) collective-permute-start(f32[256,128]{0,1:T(8,128)} %get-tuple-element.11), channel_id=1, source_target_pairs={{0,3},{1,0},{2,1},{3,2},{4,7},{5,4},{6,5},{7,6},{8,11},{9,8},{10,9... | collective-permute-start | bytes 393224 | tf_op jit(solution)/shard_map/ppermute | solution.py:10
  169.2 10.3 %copy-start.7 = (pred[256]{0:T(512)(128)(4,1)S(1)}, pred[256]{0:T(512)(128)(4,1)}, u32[]{:S(2)}) copy-start(pred[256]{0:T(512)(128)(4,1)} %compare_and_fusion.3) | copy-start | bytes 772
  173.8 9.7 %copy-start.5 = (pred[256]{0:T(512)(128)(4,1)S(1)}, pred[256]{0:T(512)(128)(4,1)}, u32[]{:S(2)}) copy-start(pred[256]{0:T(512)(128)(4,1)} %compare_and_fusion) | copy-start | bytes 772
where the time goes:
time: 227 us; the launch traced here: 226 us
  blocking collectives  160 us (70%)
  local copies, waits for them, and re-layouts  28.1 us (12%)
  other arithmetic  15.7 us (7%)
  starting transfers between devices  15.5 us (7%)
  matrix products  4.13 us (2%)
    all_gather x1, blocking collectives, on_device(): values = lax.all_gather(coarse_load, ('sub', 'col'), axis=0, tiled=True)  41.2 us
    psum x1, blocking collectives, inner(): lax.psum(0.5 * jnp.sum(left_field * right_field, axis=0), ('sub', 'col'))  39.9 us
    unnamed x1, blocking collectives  37.7 us
    all_gather x1, blocking collectives, on_device(): piece = lax.all_gather(block_rows, 'sub', axis=0, tiled=True)  30.5 us
    gather x24, local copies, waits for them, and re-layouts, combine(): jnp.take(incoming[number].astype(jnp.float32), places[number], axis=0)  16 us
    ppermute x12, starting transfers between devices, from_behind(): return lax.ppermute(value, axis, pairs)  15.5 us
    psum x1, blocking collectives, on_device(): block_rows = lax.psum(partial_rows, 'col').astype(jnp.bfloat16)  10.3 us
    select_n x14, other arithmetic, combine(): jnp.take(incoming[number].astype(jnp.float32), places[number], axis=0)  8.71 us
  transfers between devices with their start and end apart: 12, of which 1 were waited for; matrix products, arithmetic and copies ran while one was open for 12% of the time, Pallas kernels for 0%

commit v1 on v0

v1 whole, which is shorter than its diff:
```python
import functools
import math

import jax
import jax.numpy as jnp
from jax import lax
from jax.experimental import pallas as pl
from jax.experimental.pallas import tpu as pltpu
from jax.sharding import PartitionSpec as P

MESH = pl.DeviceIdType.MESH
F32 = jnp.float32
BF16 = jnp.bfloat16


def kernel(
    subs, cols,
    rhs_hbm, schur_hbm, inverse_hbm, basis_ref, coarse_ref, index_ref, links_ref,
    out_ref,
    rhs_ref, schur_ref, inverse_ref, picks, halo_rhs, halo_z, weighted, z_ref, z_half, first_ref, p_half,
    indices, chosen, arrived, columns, rows_ref, loads, sums,
    local_sem, halo_send, halo_recv, z_send, z_recv, all_send, all_recv,
):
    count = subs * cols
    row = lax.axis_index("sub")
    column = lax.axis_index("col")
    me = row * cols + column
    size = rhs_ref.shape[0]
    face = size // 4
    primals = index_ref.shape[1]
    height, width = coarse_ref.shape
    group = math.gcd(count, 32)

    def place(target):
        return (target // cols, target % cols)

    neighbours = (
        ((row + subs - 1) % subs, column),
        ((row + 1) % subs, column),
        (row, (column + cols - 1) % cols),
        (row, (column + 1) % cols),
    )

    barrier = pltpu.get_barrier_semaphore()

    def greet(step, carry):
        pl.semaphore_signal(
            barrier, inc=1, device_id=place((me + step) % count), device_id_type=MESH
        )
        return carry

    lax.fori_loop(1, count, greet, 0)

    load_rhs = pltpu.make_async_copy(rhs_hbm.at[0], rhs_ref, local_sem.at[0])
    load_inverse = pltpu.make_async_copy(inverse_hbm.at[0], inverse_ref, local_sem.at[1])
    load_schur = pltpu.make_async_copy(schur_hbm.at[0], schur_ref, local_sem.at[2])
    load_rhs.start()
    load_inverse.start()
    load_schur.start()

    lanes = indices.shape[2]
    indices[me] = jnp.zeros((1, lanes), F32)
    indices[me, :, pl.ds(0, primals)] = index_ref[...].astype(F32)

    offsets = (face, 0, 3 * face, 2 * face)
    for f in range(4):
        places = links_ref[:, f * face : (f + 1) * face] - offsets[f]
        hit = lax.broadcasted_iota(jnp.int32, (face, face), 0) == places
        picks[f] = jnp.where(hit, 1.0, 0.0).astype(F32).T.astype(BF16)

    pl.semaphore_wait(barrier, count - 1)

    def halo_copies(source, target, send, recv):
        copies = []
        for g in range(4):
            copies.append(
                pltpu.make_async_remote_copy(
                    src_ref=source(g),
                    dst_ref=target.at[g ^ 1],
                    send_sem=send.at[g],
                    recv_sem=recv.at[g ^ 1],
                    device_id=neighbours[g],
                    device_id_type=MESH,
                )
            )
        return copies

    def broadcast(slots, number):
        def send(step, carry):
            pltpu.make_async_remote_copy(
                src_ref=slots.at[me],
                dst_ref=slots.at[me],
                send_sem=all_send.at[number],
                recv_sem=all_recv.at[number],
                device_id=place((me + step) % count),
                device_id_type=MESH,
            ).start()
            return carry

        lax.fori_loop(1, count, send, 0)

    def wait_all(slots, sems, number):
        part = slots.at[pl.ds(0, count - 1)]
        pltpu.make_async_copy(part, part, sems.at[number]).wait()

    rhs_copies = halo_copies(
        lambda g: rhs_hbm.at[0, pl.ds(g * face, face)], halo_rhs, halo_send, halo_recv
    )
    for copy in rhs_copies:
        copy.start()
    broadcast(indices, 0)

    basis = basis_ref[0]
    basis_t = basis.astype(F32).T.astype(BF16)
    load_rhs.wait()

    for copy in rhs_copies:
        copy.wait_recv()
    for f in range(4):
        block = pl.ds(f * face, face)
        got = jnp.dot(picks[f], halo_rhs[f], preferred_element_type=F32)
        residual = rhs_ref[block, :].astype(F32) + got
        first_ref[block, :] = residual
        weighted[block, :] = (residual * 0.5).astype(BF16)
    loads[me] = jnp.dot(basis, weighted[...], preferred_element_type=F32).astype(BF16)
    broadcast(loads, 1)

    wait_all(indices, all_recv, 0)

    def spread(g, extent):
        values = indices[pl.ds(g * group, group)]
        values = jnp.broadcast_to(values, (group, primals, lanes))
        diagonal = lax.broadcasted_iota(jnp.int32, values.shape, 1) == lax.broadcasted_iota(
            jnp.int32, values.shape, 2
        )
        named = jnp.sum(jnp.where(diagonal, values, 0.0), axis=2, keepdims=True)
        named = named.astype(jnp.int32)
        return jnp.broadcast_to(named, (group, primals, extent))

    def choose(g, carry):
        named = spread(g, height) - row * height
        hit = lax.broadcasted_iota(jnp.int32, named.shape, 2) == named
        hit = jnp.where(hit, 1.0, 0.0).astype(F32).reshape(group * primals, height).astype(BF16)
        picked = jnp.dot(hit, coarse_ref[...], preferred_element_type=F32)
        chosen[pl.ds(g * group, group)] = picked.reshape(group, primals, width).astype(BF16)
        return carry

    lax.fori_loop(0, count // group, choose, 0)
    arrived[me] = chosen[me]

    def send_rows(step, carry):
        target = (me + step) % count
        pltpu.make_async_remote_copy(
            src_ref=chosen.at[target],
            dst_ref=arrived.at[me],
            send_sem=all_send.at[2],
            recv_sem=all_recv.at[2],
            device_id=place(target),
            device_id_type=MESH,
        ).start()
        return carry

    lax.fori_loop(1, count, send_rows, 0)

    load_inverse.wait()
    for f in range(4):
        block = pl.ds(f * face, face)
        z_ref[block, :] = jnp.dot(inverse_ref[block, :], weighted[...], preferred_element_type=F32)

    wait_all(arrived, all_recv, 2)
    for j in range(cols):
        def add(i, total):
            return total + arrived[i * cols + j].astype(F32)

        rows_ref[j] = lax.fori_loop(0, subs, add, jnp.zeros((primals, width), F32), unroll=subs <= 8)

    def arrange(g, carry):
        total = jnp.zeros((primals, group * primals), F32)
        for j in range(cols):
            named = spread(g, width) - j * width
            hit = lax.broadcasted_iota(jnp.int32, named.shape, 2) == named
            hit = jnp.where(hit, 1.0, 0.0).astype(F32).reshape(group * primals, width).astype(BF16)
            total += lax.dot_general(
                rows_ref[j].astype(BF16), hit, (((1,), (1,)), ((), ())), preferred_element_type=F32
            )
        columns[g] = total
        return carry

    lax.fori_loop(0, count // group, arrange, 0)

    wait_all(loads, all_recv, 1)

    def solve(g, total):
        part = loads[pl.ds(g * group, group)].astype(F32).reshape(group * primals, loads.shape[2])
        return total + jnp.dot(columns[g].astype(BF16), part.astype(BF16), preferred_element_type=F32)

    taken = lax.fori_loop(
        0, count // group, solve, jnp.zeros((primals, loads.shape[2]), F32)
    ).astype(BF16)

    correction = jnp.dot(basis_t, taken, preferred_element_type=F32)
    z_value = (z_ref[...] + correction) * 0.5
    z_ref[...] = z_value
    z_half[...] = z_value.astype(BF16)
    z_copies = halo_copies(lambda g: z_half.at[pl.ds(g * face, face)], halo_z, z_send, z_recv)
    for copy in z_copies:
        copy.start()
    sums[me, pl.ds(0, 1), :] = jnp.sum(first_ref[...] * z_ref[...], axis=0, keepdims=True)
    load_schur.wait()
    for copy in z_copies:
        copy.wait_recv()
    for f in range(4):
        block = pl.ds(f * face, face)
        first = z_ref[block, :] + jnp.dot(picks[f], halo_z[f], preferred_element_type=F32)
        first_ref[block, :] = first
        p_half[block, :] = first.astype(BF16)
    total = jnp.zeros((1, first_ref.shape[1]), F32)
    for f in range(4):
        block = pl.ds(f * face, face)
        image = jnp.dot(schur_ref[block, :], p_half[...], preferred_element_type=F32)
        total += jnp.sum(first_ref[block, :] * image, axis=0, keepdims=True)
    sums[me, pl.ds(1, 1), :] = total
    broadcast(sums, 3)

    for copy in rhs_copies + z_copies:
        copy.wait_send()
    wait_all(indices, all_send, 0)
    wait_all(loads, all_send, 1)
    wait_all(arrived, all_send, 2)
    wait_all(sums, all_recv, 3)
    whole = jnp.sum(sums[...], axis=0)
    alpha = whole[0:1, :] / whole[1:2, :]
    out_ref[0] = (alpha * first_ref[...]).astype(BF16)
    wait_all(sums, all_send, 3)


def solution(mesh):
    subs, cols = mesh.shape["sub"], mesh.shape["col"]
    count = subs * cols

    def step(rhs, schur, local_inverse, basis, coarse_inverse, primal_index, neighbour_dof):
        size, cases = rhs.shape[1:]
        face = size // 4
        primals = primal_index.shape[1]
        height, width = coarse_inverse.shape
        lanes = 128 * pl.cdiv(primals, 128)
        group = math.gcd(count, 32)
        anywhere = pl.BlockSpec(memory_space=pl.ANY)
        near = pl.BlockSpec(memory_space=pltpu.VMEM)
        return pl.pallas_call(
            functools.partial(kernel, subs, cols),
            out_shape=jax.ShapeDtypeStruct(rhs.shape, BF16),
            in_specs=[anywhere] * 3 + [near] * 4,
            out_specs=near,
            scratch_shapes=[
                pltpu.VMEM((size, cases), BF16),
                pltpu.VMEM((size, size), BF16),
                pltpu.VMEM((size, size), BF16),
                pltpu.VMEM((4, face, face), BF16),
                pltpu.VMEM((4, face, cases), BF16),
                pltpu.VMEM((4, face, cases), BF16),
                pltpu.VMEM((size, cases), BF16),
                pltpu.VMEM((size, cases), F32),
                pltpu.VMEM((size, cases), BF16),
                pltpu.VMEM((size, cases), F32),
                pltpu.VMEM((size, cases), BF16),
                pltpu.VMEM((count, 1, lanes), F32),
                pltpu.VMEM((count, primals, width), BF16),
                pltpu.VMEM((count, primals, width), BF16),
                pltpu.VMEM((count // group, primals, group * primals), F32),
                pltpu.VMEM((cols, primals, width), F32),
                pltpu.VMEM((count, primals, cases), BF16),
                pltpu.VMEM((count, 2, cases), F32),
                pltpu.SemaphoreType.DMA((3,)),
                pltpu.SemaphoreType.DMA((4,)),
                pltpu.SemaphoreType.DMA((4,)),
                pltpu.SemaphoreType.DMA((4,)),
                pltpu.SemaphoreType.DMA((4,)),
                pltpu.SemaphoreType.DMA((4,)),
                pltpu.SemaphoreType.DMA((4,)),
            ],
            compiler_params=pltpu.CompilerParams(
                collective_id=0, has_side_effects=True, vmem_limit_bytes=60 * 1024 * 1024
            ),
        )(rhs, schur, local_inverse, basis, coarse_inverse, primal_index, neighbour_dof)

    return jax.shard_map(
        step,
        mesh=mesh,
        in_specs=(
            P(("sub", "col"), None, None),
            P(("sub", "col"), None, None),
            P(("sub", "col"), None, None),
            P(("sub", "col"), None, None),
            P("sub", "col"),
            P(("sub", "col"), None),
            P(("sub", "col"), None),
        ),
        out_specs=P(("sub", "col"), None, None),
        check_vma=False,
    )
```

time: 227 us -> 32.8 us (0.14)
  blocking collectives: 160 us -> 0 us
  Pallas kernels: 0 us -> 30.9 us
  local copies, waits for them, and re-layouts: 28.1 us -> 1.67 us
  other arithmetic: 15.7 us -> 0 us
  starting transfers between devices: 15.5 us -> 0 us
  matrix products: 4.13 us -> 0 us
    all_gather x2 -> x0, blocking collectives: 71.7 us -> none  [the longest x1 41.2 us: on_device(): values = lax.all_gather(coarse_load, ('sub', 'col'), axis=0, tiled=True)]
    psum x2 -> x0, blocking collectives: 50.3 us -> none  [the longest x1 39.9 us: inner(): lax.psum(0.5 * jnp.sum(left_field * right_field, axis=0), ('sub', 'col'))]
    unnamed x1 -> x0, blocking collectives: 37.7 us -> none
    pallas_call x0 -> x1, Pallas kernels: none -> 30.9 us  [step(): pl.pallas_call(functools.partial(kernel, subs, cols), out_shape=jax.Shape...]
    gather x25 -> x0, local copies, waits for them, and re-layouts: 16.7 us -> none  [the longest x24 16 us: combine(): jnp.take(incoming[number].astype(jnp.float32), places[number], axis=0)]
    ppermute x12 -> x0, starting transfers between devices: 15.5 us -> none  [from_behind(): return lax.ppermute(value, axis, pairs)]
    select_n x16 -> x0, other arithmetic: 9.3 us -> none  [the longest x14 8.71 us: combine(): jnp.take(incoming[number].astype(jnp.float32), places[number], axis=0)]
    ppermute x9 -> x0, local copies, waits for them, and re-layouts: 4.41 us -> none  [from_behind(): return lax.ppermute(value, axis, pairs)]
  transfers between devices with their start and end apart: 12 -> 0, of which waited for: 1 -> 0; matrix products, arithmetic and copies ran while one was open for 12% -> 0% of each run, Pallas kernels for 0% -> 0%
where the time goes in v1:
time: 32.8 us; the launch traced here: 32.6 us
  Pallas kernels  30.9 us (94%)
  local copies, waits for them, and re-layouts  1.67 us (5%)
    pallas_call x1, Pallas kernels, step(): pl.pallas_call(functools.partial(kernel, subs, cols), out_shape=jax.Shape...  30.9 us
    unnamed x1, local copies, waits for them, and re-layouts  1.67 us

profile of v1, /device:TPU:0, one launch (start us, length us, event | category | flops | bytes accessed | tf_op | source)
XLA Modules:
  0.0 32.6 jit_solution(4882694122241761353)
XLA Ops:
  0.0 30.9 %shard_map.73 = bf16[1,1024,128]{2,1,0:T(8,128)(2,1)} custom-call(bf16[1,1024,128]{2,1,0:T(8,128)(2,1)} %rhs_hbm.1, bf16[1,1024,1024]{2,1,0:T(8,128)(2,1)} %schur_hbm.1, bf16[1,1024,1024]{2,1,0:T(8,128)(2,1)} %inverse_hbm.1, bf16[1,8,1024]{2,1,0:T(8,128)(2,1)} %basis_ref.1, bf16[32,64]{1,0:T(8,128)(2,1)} %coarse_ref.1, s32[1,8]{1,0:T(1,128)} %index_ref.1, ...), custom_call_target="tpu_custom_call" | custom-call | tf_op jit(solution)/shard_map/pallas_call | solution.py:250
  30.9 1.7 %copy.9 = bf16[1,1024,128]{2,1,0:T(8,128)(2,1)} copy(bf16[1,1024,128]{2,1,0:T(8,128)(2,1)} %shard_map.73) | data formatting | bytes 524288

commit v2 on v1

--- a/solution.py
+++ b/solution.py
@@ -11,14 +11,16 @@
 MESH = pl.DeviceIdType.MESH
 F32 = jnp.float32
 BF16 = jnp.bfloat16
+UNROLL = False
 
 
 def kernel(
     subs, cols,
-    rhs_hbm, schur_hbm, inverse_hbm, basis_ref, coarse_ref, index_ref, links_ref,
-    out_ref,
+    rhs_hbm, schur_hbm, inverse_hbm, basis_hbm, coarse_hbm, index_hbm, links_hbm,
+    first_out, alpha_ref,
+    basis_ref, coarse_ref, index_ref, links_ref,
     rhs_ref, schur_ref, inverse_ref, picks, halo_rhs, halo_z, weighted, z_ref, z_half, first_ref, p_half,
-    indices, chosen, arrived, columns, rows_ref, loads, sums,
+    image_ref, indices, chosen, arrived, vector, loads, sums,
     local_sem, halo_send, halo_recv, z_send, z_recv, all_send, all_recv,
 ):
     count = subs * cols
@@ -41,22 +43,46 @@
         (row, (column + 1) % cols),
     )
 
+    half_way = (row * 2) // subs
+
+    def each_other(act):
+        def body(step, carry):
+            q = step // cols
+            target_row = (1 - half_way) * (subs - 1 - q) + half_way * q
+            target = target_row * cols + (column + step) % cols
+
+            @pl.when(target != me)
+            def _():
+                act(target)
+
+            return carry
+
+        lax.fori_loop(0, count, body, 0, unroll=UNROLL and count <= 64)
+
     barrier = pltpu.get_barrier_semaphore()
 
-    def greet(step, carry):
-        pl.semaphore_signal(
-            barrier, inc=1, device_id=place((me + step) % count), device_id_type=MESH
-        )
-        return carry
-
-    lax.fori_loop(1, count, greet, 0)
-
+    each_other(
+        lambda target: pl.semaphore_signal(
+            barrier, inc=1, device_id=place(target), device_id_type=MESH
+        )
+    )
+
+    small_loads = [
+        pltpu.make_async_copy(source, target, local_sem.at[4 + number])
+        for number, (source, target) in enumerate(
+            ((links_hbm, links_ref), (index_hbm, index_ref), (basis_hbm, basis_ref), (coarse_hbm, coarse_ref))
+        )
+    ]
+    for load in small_loads:
+        load.start()
     load_rhs = pltpu.make_async_copy(rhs_hbm.at[0], rhs_ref, local_sem.at[0])
     load_inverse = pltpu.make_async_copy(inverse_hbm.at[0], inverse_ref, local_sem.at[1])
     load_schur = pltpu.make_async_copy(schur_hbm.at[0], schur_ref, local_sem.at[2])
     load_rhs.start()
     load_inverse.start()
     load_schur.start()
+    for load in small_loads:
+        load.wait()
 
     lanes = indices.shape[2]
     indices[me] = jnp.zeros((1, lanes), F32)
@@ -86,18 +112,16 @@
         return copies
 
     def broadcast(slots, number):
-        def send(step, carry):
-            pltpu.make_async_remote_copy(
+        each_other(
+            lambda target: pltpu.make_async_remote_copy(
                 src_ref=slots.at[me],
                 dst_ref=slots.at[me],
                 send_sem=all_send.at[number],
                 recv_sem=all_recv.at[number],
-                device_id=place((me + step) % count),
+                device_id=place(target),
                 device_id_type=MESH,
             ).start()
-            return carry
-
-        lax.fori_loop(1, count, send, 0)
+        )
 
     def wait_all(slots, sems, number):
         part = slots.at[pl.ds(0, count - 1)]
@@ -114,15 +138,17 @@
     basis_t = basis.astype(F32).T.astype(BF16)
     load_rhs.wait()
 
-    for copy in rhs_copies:
-        copy.wait_recv()
-    for f in range(4):
+    load = jnp.zeros((primals, rhs_ref.shape[1]), F32)
+    for f in (2, 3, 0, 1):
         block = pl.ds(f * face, face)
+        rhs_copies[f ^ 1].wait_recv()
         got = jnp.dot(picks[f], halo_rhs[f], preferred_element_type=F32)
         residual = rhs_ref[block, :].astype(F32) + got
         first_ref[block, :] = residual
-        weighted[block, :] = (residual * 0.5).astype(BF16)
-    loads[me] = jnp.dot(basis, weighted[...], preferred_element_type=F32).astype(BF16)
+        part = (residual * 0.5).astype(BF16)
+        weighted[block, :] = part
+        load += jnp.dot(basis[:, f * face : (f + 1) * face], part, preferred_element_type=F32)
+    loads[me] = load.astype(BF16)
     broadcast(loads, 1)
 
     wait_all(indices, all_recv, 0)
@@ -148,9 +174,8 @@
     lax.fori_loop(0, count // group, choose, 0)
     arrived[me] = chosen[me]
 
-    def send_rows(step, carry):
-        target = (me + step) % count
-        pltpu.make_async_remote_copy(
+    each_other(
+        lambda target: pltpu.make_async_remote_copy(
             src_ref=chosen.at[target],
             dst_ref=arrived.at[me],
             send_sem=all_send.at[2],
@@ -158,69 +183,77 @@
             device_id=place(target),
             device_id_type=MESH,
         ).start()
-        return carry
-
-    lax.fori_loop(1, count, send_rows, 0)
+    )
 
     load_inverse.wait()
     for f in range(4):
         block = pl.ds(f * face, face)
         z_ref[block, :] = jnp.dot(inverse_ref[block, :], weighted[...], preferred_element_type=F32)
 
-    wait_all(arrived, all_recv, 2)
-    for j in range(cols):
-        def add(i, total):
-            return total + arrived[i * cols + j].astype(F32)
-
-        rows_ref[j] = lax.fori_loop(0, subs, add, jnp.zeros((primals, width), F32), unroll=subs <= 8)
-
-    def arrange(g, carry):
-        total = jnp.zeros((primals, group * primals), F32)
+    wait_all(loads, all_recv, 1)
+    vector[...] = jnp.zeros_like(vector)
+
+    def gather(g, carry):
+        part = loads[pl.ds(g * group, group)].astype(F32).reshape(group * primals, loads.shape[2])
+        part = part.astype(BF16)
         for j in range(cols):
             named = spread(g, width) - j * width
             hit = lax.broadcasted_iota(jnp.int32, named.shape, 2) == named
             hit = jnp.where(hit, 1.0, 0.0).astype(F32).reshape(group * primals, width).astype(BF16)
-            total += lax.dot_general(
-                rows_ref[j].astype(BF16), hit, (((1,), (1,)), ((), ())), preferred_element_type=F32
+            vector[j] += lax.dot_general(
+                hit, part, (((0,), (0,)), ((), ())), preferred_element_type=F32
             )
-        columns[g] = total
         return carry
 
-    lax.fori_loop(0, count // group, arrange, 0)
-
-    wait_all(loads, all_recv, 1)
-
-    def solve(g, total):
-        part = loads[pl.ds(g * group, group)].astype(F32).reshape(group * primals, loads.shape[2])
-        return total + jnp.dot(columns[g].astype(BF16), part.astype(BF16), preferred_element_type=F32)
-
-    taken = lax.fori_loop(
-        0, count // group, solve, jnp.zeros((primals, loads.shape[2]), F32)
-    ).astype(BF16)
-
-    correction = jnp.dot(basis_t, taken, preferred_element_type=F32)
-    z_value = (z_ref[...] + correction) * 0.5
-    z_ref[...] = z_value
-    z_half[...] = z_value.astype(BF16)
+    lax.fori_loop(0, count // group, gather, 0)
+
+    wait_all(arrived, all_recv, 2)
+    taken = jnp.zeros((primals, loads.shape[2]), F32)
+    for j in range(cols):
+        def add(i, total):
+            return total + arrived[i * cols + j].astype(F32)
+
+        rows = lax.fori_loop(0, subs, add, jnp.zeros((primals, width), F32), unroll=subs <= 8)
+        taken += jnp.dot(rows.astype(BF16), vector[j].astype(BF16), preferred_element_type=F32)
+    taken = taken.astype(BF16)
+
     z_copies = halo_copies(lambda g: z_half.at[pl.ds(g * face, face)], halo_z, z_send, z_recv)
-    for copy in z_copies:
-        copy.start()
+    for f in range(4):
+        block = pl.ds(f * face, face)
+        correction = jnp.dot(
+            basis_t[f * face : (f + 1) * face, :], taken, preferred_element_type=F32
+        )
+        z_value = (z_ref[block, :] + correction) * 0.5
+        z_ref[block, :] = z_value
+        z_half[block, :] = z_value.astype(BF16)
+        z_copies[f].start()
     sums[me, pl.ds(0, 1), :] = jnp.sum(first_ref[...] * z_ref[...], axis=0, keepdims=True)
     load_schur.wait()
-    for copy in z_copies:
-        copy.wait_recv()
-    for f in range(4):
-        block = pl.ds(f * face, face)
-        first = z_ref[block, :] + jnp.dot(picks[f], halo_z[f], preferred_element_type=F32)
-        first_ref[block, :] = first
-        p_half[block, :] = first.astype(BF16)
+    for pair in ((2, 3), (0, 1)):
+        for f in pair:
+            block = pl.ds(f * face, face)
+            z_copies[f ^ 1].wait_recv()
+            first = z_ref[block, :] + jnp.dot(picks[f], halo_z[f], preferred_element_type=F32)
+            first_ref[block, :] = first
+            p_half[block, :] = first.astype(BF16)
+        both = pl.ds(pair[0] * face, 2 * face)
+        if pair[0] == 2:
+            for f in range(4):
+                block = pl.ds(f * face, face)
+                image_ref[block, :] = jnp.dot(
+                    schur_ref[block, both], p_half[both, :], preferred_element_type=F32
+                )
     total = jnp.zeros((1, first_ref.shape[1]), F32)
     for f in range(4):
         block = pl.ds(f * face, face)
-        image = jnp.dot(schur_ref[block, :], p_half[...], preferred_element_type=F32)
+        image = image_ref[block, :] + jnp.dot(
+            schur_ref[block, both], p_half[both, :], preferred_element_type=F32
+        )
         total += jnp.sum(first_ref[block, :] * image, axis=0, keepdims=True)
     sums[me, pl.ds(1, 1), :] = total
     broadcast(sums, 3)
+    store = pltpu.make_async_copy(first_ref, first_out, local_sem.at[3])
+    store.start()
 
     for copy in rhs_copies + z_copies:
         copy.wait_send()
@@ -229,8 +262,8 @@
     wait_all(arrived, all_send, 2)
     wait_all(sums, all_recv, 3)
     whole = jnp.sum(sums[...], axis=0)
-    alpha = whole[0:1, :] / whole[1:2, :]
-    out_ref[0] = (alpha * first_ref[...]).astype(BF16)
+    alpha_ref[...] = whole[0:1, :] / whole[1:2, :]
+    store.wait()
     wait_all(sums, all_send, 3)
 
 
@@ -244,15 +277,21 @@
         primals = primal_index.shape[1]
         height, width = coarse_inverse.shape
         lanes = 128 * pl.cdiv(primals, 128)
-        group = math.gcd(count, 32)
         anywhere = pl.BlockSpec(memory_space=pl.ANY)
         near = pl.BlockSpec(memory_space=pltpu.VMEM)
-        return pl.pallas_call(
+        first, alpha = pl.pallas_call(
             functools.partial(kernel, subs, cols),
-            out_shape=jax.ShapeDtypeStruct(rhs.shape, BF16),
-            in_specs=[anywhere] * 3 + [near] * 4,
-            out_specs=near,
+            out_shape=(
+                jax.ShapeDtypeStruct((size, cases), F32),
+                jax.ShapeDtypeStruct((1, cases), F32),
+            ),
+            in_specs=[anywhere] * 7,
+            out_specs=(anywhere, near),
             scratch_shapes=[
+                pltpu.VMEM(basis.shape, BF16),
+                pltpu.VMEM(coarse_inverse.shape, BF16),
+                pltpu.VMEM(primal_index.shape, jnp.int32),
+                pltpu.VMEM(neighbour_dof.shape, jnp.int32),
                 pltpu.VMEM((size, cases), BF16),
                 pltpu.VMEM((size, size), BF16),
                 pltpu.VMEM((size, size), BF16),
@@ -264,14 +303,14 @@
                 pltpu.VMEM((size, cases), BF16),
                 pltpu.VMEM((size, cases), F32),
                 pltpu.VMEM((size, cases), BF16),
+                pltpu.VMEM((size, cases), F32),
                 pltpu.VMEM((count, 1, lanes), F32),
                 pltpu.VMEM((count, primals, width), BF16),
                 pltpu.VMEM((count, primals, width), BF16),
-                pltpu.VMEM((count // group, primals, group * primals), F32),
-                pltpu.VMEM((cols, primals, width), F32),
+                pltpu.VMEM((cols, width, cases), F32),
                 pltpu.VMEM((count, primals, cases), BF16),
                 pltpu.VMEM((count, 2, cases), F32),
-                pltpu.SemaphoreType.DMA((3,)),
+                pltpu.SemaphoreType.DMA((8,)),
                 pltpu.SemaphoreType.DMA((4,)),
                 pltpu.SemaphoreType.DMA((4,)),
                 pltpu.SemaphoreType.DMA((4,)),
@@ -283,6 +322,7 @@
                 collective_id=0, has_side_effects=True, vmem_limit_bytes=60 * 1024 * 1024
             ),
         )(rhs, schur, local_inverse, basis, coarse_inverse, primal_index, neighbour_dof)
+        return (alpha * first).astype(BF16)[None]
 
     return jax.shard_map(
         step,

time: 32.8 us -> 31.4 us (0.957)
  other arithmetic: 0 us -> 1.78 us
  local copies, waits for them, and re-layouts: 1.67 us -> 0 us
  Pallas kernels: 30.9 us -> 29.5 us
    broadcast_in_dim x0 -> x1, other arithmetic: none -> 1.78 us  [step(): return (alpha * first).astype(BF16)[None]]
    unnamed x1 -> x0, local copies, waits for them, and re-layouts: 1.67 us -> none
    pallas_call x1, Pallas kernels: 30.9 us -> 29.5 us  [step(): pl.pallas_call(functools.partial(kernel, subs, cols), out_shape=(jax.Shap...]
where the time goes in v2:
time: 31.4 us; the launch traced here: 31.3 us
  Pallas kernels  29.5 us (94%)
  other arithmetic  1.78 us (6%)
    pallas_call x1, Pallas kernels, step(): pl.pallas_call(functools.partial(kernel, subs, cols), out_shape=(jax.Shap...  29.5 us
    broadcast_in_dim x1, other arithmetic, step(): return (alpha * first).astype(BF16)[None]  1.78 us

profile of v2, /device:TPU:0, one launch (start us, length us, event | category | flops | bytes accessed | tf_op | source)
XLA Modules:
  0.0 31.3 jit_solution(4517281932634445083)
XLA Ops:
  0.0 29.5 %shard_map.73 = (f32[1024,128]{1,0:T(8,128)}, f32[1,128]{1,0:T(1,128)}) custom-call(bf16[1,1024,128]{2,1,0:T(8,128)(2,1)} %rhs_hbm.1, bf16[1,1024,1024]{2,1,0:T(8,128)(2,1)} %schur_hbm.1, bf16[1,1024,1024]{2,1,0:T(8,128)(2,1)} %inverse_hbm.1, bf16[1,8,1024]{2,1,0:T(8,128)(2,1)} %basis_hbm.1, bf16[32,64]{1,0:T(8,128)(2,1)} %coarse_hbm.1, s32[1,8]{1,0:T(1,128)} %index_hbm.1, ...), custom_call_target="tpu_custom_call" | custom-call | tf_op jit(solution)/shard_map/pallas_call | solution.py:282
  29.5 1.8 %fusion = bf16[1,1024,128]{2,1,0:T(8,128)(2,1)} fusion(f32[1024,128]{1,0:T(8,128)} %get-tuple-element.8, f32[128]{0:T(128)} %bitcast.3), kind=kLoop, calls=%fused_computation.1 | loop fusion | flops 262144 | bytes 786944 | tf_op jit(solution)/shard_map/broadcast_in_dim | solution.py:325

commit v3 on v2

--- a/solution.py
+++ b/solution.py
@@ -11,15 +11,15 @@
 MESH = pl.DeviceIdType.MESH
 F32 = jnp.float32
 BF16 = jnp.bfloat16
-UNROLL = False
+UNROLL = True
 
 
 def kernel(
     subs, cols,
     rhs_hbm, schur_hbm, inverse_hbm, basis_hbm, coarse_hbm, index_hbm, links_hbm,
-    first_out, alpha_ref,
+    first_ref, alpha_ref,
     basis_ref, coarse_ref, index_ref, links_ref,
-    rhs_ref, schur_ref, inverse_ref, picks, halo_rhs, halo_z, weighted, z_ref, z_half, first_ref, p_half,
+    rhs_ref, schur_ref, inverse_ref, picks, halo_rhs, halo_z, weighted, z_ref, z_half, p_half,
     image_ref, indices, chosen, arrived, vector, loads, sums,
     local_sem, halo_send, halo_recv, z_send, z_recv, all_send, all_recv,
 ):
@@ -36,13 +36,6 @@
     def place(target):
         return (target // cols, target % cols)
 
-    neighbours = (
-        ((row + subs - 1) % subs, column),
-        ((row + 1) % subs, column),
-        (row, (column + cols - 1) % cols),
-        (row, (column + 1) % cols),
-    )
-
     half_way = (row * 2) // subs
 
     def each_other(act):
@@ -96,20 +89,31 @@
 
     pl.semaphore_wait(barrier, count - 1)
 
+    swap = row % 2
+
     def halo_copies(source, target, send, recv):
         copies = []
-        for g in range(4):
+        for g in (swap, 1 - swap, 2, 3):
+            if isinstance(g, int):
+                facing = 5 - g
+                partner = (row, (column + cols + 2 * g - 5) % cols)
+            else:
+                facing = 1 - g
+                partner = ((row + subs + 2 * g - 1) % subs, column)
             copies.append(
                 pltpu.make_async_remote_copy(
                     src_ref=source(g),
-                    dst_ref=target.at[g ^ 1],
+                    dst_ref=target.at[facing],
                     send_sem=send.at[g],
-                    recv_sem=recv.at[g ^ 1],
-                    device_id=neighbours[g],
+                    recv_sem=recv.at[facing],
+                    device_id=partner,
                     device_id_type=MESH,
                 )
             )
         return copies
+
+    def wait_face(target, recv, f):
+        pltpu.make_async_copy(target.at[f], target.at[f], recv.at[f]).wait()
 
     def broadcast(slots, number):
         each_other(
@@ -141,7 +145,7 @@
     load = jnp.zeros((primals, rhs_ref.shape[1]), F32)
     for f in (2, 3, 0, 1):
         block = pl.ds(f * face, face)
-        rhs_copies[f ^ 1].wait_recv()
+        wait_face(halo_rhs, halo_recv, f)
         got = jnp.dot(picks[f], halo_rhs[f], preferred_element_type=F32)
         residual = rhs_ref[block, :].astype(F32) + got
         first_ref[block, :] = residual
@@ -226,13 +230,17 @@
         z_value = (z_ref[block, :] + correction) * 0.5
         z_ref[block, :] = z_value
         z_half[block, :] = z_value.astype(BF16)
-        z_copies[f].start()
+        if f == 1:
+            z_copies[0].start()
+            z_copies[1].start()
+        if f > 1:
+            z_copies[f].start()
     sums[me, pl.ds(0, 1), :] = jnp.sum(first_ref[...] * z_ref[...], axis=0, keepdims=True)
     load_schur.wait()
     for pair in ((2, 3), (0, 1)):
         for f in pair:
             block = pl.ds(f * face, face)
-            z_copies[f ^ 1].wait_recv()
+            wait_face(halo_z, z_recv, f)
             first = z_ref[block, :] + jnp.dot(picks[f], halo_z[f], preferred_element_type=F32)
             first_ref[block, :] = first
             p_half[block, :] = first.astype(BF16)
@@ -252,9 +260,6 @@
         total += jnp.sum(first_ref[block, :] * image, axis=0, keepdims=True)
     sums[me, pl.ds(1, 1), :] = total
     broadcast(sums, 3)
-    store = pltpu.make_async_copy(first_ref, first_out, local_sem.at[3])
-    store.start()
-
     for copy in rhs_copies + z_copies:
         copy.wait_send()
     wait_all(indices, all_send, 0)
@@ -263,7 +268,6 @@
     wait_all(sums, all_recv, 3)
     whole = jnp.sum(sums[...], axis=0)
     alpha_ref[...] = whole[0:1, :] / whole[1:2, :]
-    store.wait()
     wait_all(sums, all_send, 3)
 
 
@@ -277,8 +281,12 @@
         primals = primal_index.shape[1]
         height, width = coarse_inverse.shape
         lanes = 128 * pl.cdiv(primals, 128)
-        anywhere = pl.BlockSpec(memory_space=pl.ANY)
+        anywhere = pl.BlockSpec(memory_space=pltpu.HBM)
         near = pl.BlockSpec(memory_space=pltpu.VMEM)
+        fixed = 4 * size * size + 8 * face * face + 22 * size * cases
+        slots = count * (4 * 8 * lanes + 8 * primals * width + 4 * primals * cases + 4 * 8 * cases)
+        blocks = 4 * cols * width * cases
+        limit = min(fixed + slots + blocks + 4 * 1024 * 1024, 63 * 1024 * 1024)
         first, alpha = pl.pallas_call(
             functools.partial(kernel, subs, cols),
             out_shape=(
@@ -286,7 +294,7 @@
                 jax.ShapeDtypeStruct((1, cases), F32),
             ),
             in_specs=[anywhere] * 7,
-            out_specs=(anywhere, near),
+            out_specs=(near, near),
             scratch_shapes=[
                 pltpu.VMEM(basis.shape, BF16),
                 pltpu.VMEM(coarse_inverse.shape, BF16),
@@ -301,7 +309,6 @@
                 pltpu.VMEM((size, cases), BF16),
                 pltpu.VMEM((size, cases), F32),
                 pltpu.VMEM((size, cases), BF16),
-                pltpu.VMEM((size, cases), F32),
                 pltpu.VMEM((size, cases), BF16),
                 pltpu.VMEM((size, cases), F32),
                 pltpu.VMEM((count, 1, lanes), F32),
@@ -319,9 +326,9 @@
                 pltpu.SemaphoreType.DMA((4,)),
             ],
             compiler_params=pltpu.CompilerParams(
-                collective_id=0, has_side_effects=True, vmem_limit_bytes=60 * 1024 * 1024
+                collective_id=0, has_side_effects=True, vmem_limit_bytes=limit
             ),
-        )(rhs, schur, local_inverse, basis, coarse_inverse, primal_index, neighbour_dof)
+        )(*(pltpu.with_memory_space_constraint(x, pltpu.HBM) for x in (rhs, schur, local_inverse, basis, coarse_inverse, primal_index, neighbour_dof)))
         return (alpha * first).astype(BF16)[None]
 
     return jax.shard_map(

time: 31.4 us -> 29.7 us (0.946)
  other arithmetic: 1.78 us -> 0.73 us
  Pallas kernels: 29.5 us -> 28.8 us
    broadcast_in_dim x1, other arithmetic: 1.78 us -> 0.73 us  [step(): return (alpha * first).astype(BF16)[None]]
    pallas_call x1, Pallas kernels: 29.5 us -> 28.8 us  [step(): pl.pallas_call(functools.partial(kernel, subs, cols), out_shape=(jax.Shap...]
where the time goes in v3:
time: 29.7 us; the launch traced here: 29.5 us
  Pallas kernels  28.8 us (97%)
  other arithmetic  0.73 us (2%)
    pallas_call x1, Pallas kernels, step(): pl.pallas_call(functools.partial(kernel, subs, cols), out_shape=(jax.Shap...  28.8 us
    broadcast_in_dim x1, other arithmetic, step(): return (alpha * first).astype(BF16)[None]  0.73 us

profile of v3, /device:TPU:0, one launch (start us, length us, event | category | flops | bytes accessed | tf_op | source)
XLA Modules:
  0.0 29.5 jit_solution(17075802596596908561)
XLA Ops:
  0.0 28.8 %shard_map.73 = (f32[1024,128]{1,0:T(8,128)S(1)}, f32[1,128]{1,0:T(1,128)S(1)}) custom-call(bf16[1,1024,128]{2,1,0:T(8,128)(2,1)} %rhs_hbm.1, bf16[1,1024,1024]{2,1,0:T(8,128)(2,1)} %schur_hbm.1, bf16[1,1024,1024]{2,1,0:T(8,128)(2,1)} %inverse_hbm.1, bf16[1,8,1024]{2,1,0:T(8,128)(2,1)} %basis_hbm.1, bf16[32,64]{1,0:T(8,128)(2,1)} %coarse_hbm.1, ...), custom_call_target="tpu_custom_call" | custom-call | tf_op jit(solution)/shard_map/pallas_call | solution.py:290
  28.8 0.7 %fusion = bf16[1,1024,128]{2,1,0:T(8,128)(2,1)} fusion(f32[1024,128]{1,0:T(8,128)S(1)} %get-tuple-element.8, f32[128]{0:T(128)S(1)} %bitcast.3), kind=kLoop, calls=%fused_computation.1 | loop fusion | flops 262144 | bytes 786944 | tf_op jit(solution)/shard_map/broadcast_in_dim | solution.py:332

commit v4 on v3

--- a/solution.py
+++ b/solution.py
@@ -20,7 +20,7 @@
     first_ref, alpha_ref,
     basis_ref, coarse_ref, index_ref, links_ref,
     rhs_ref, schur_ref, inverse_ref, picks, halo_rhs, halo_z, weighted, z_ref, z_half, p_half,
-    image_ref, indices, chosen, arrived, vector, loads, sums,
+    image_ref, indices, chosen, arrived, columns, rows_ref, loads, sums,
     local_sem, halo_send, halo_recv, z_send, z_recv, all_send, all_recv,
 ):
     count = subs * cols
@@ -134,13 +134,47 @@
     rhs_copies = halo_copies(
         lambda g: rhs_hbm.at[0, pl.ds(g * face, face)], halo_rhs, halo_send, halo_recv
     )
+    broadcast(indices, 0)
     for copy in rhs_copies:
         copy.start()
-    broadcast(indices, 0)
 
     basis = basis_ref[0]
     basis_t = basis.astype(F32).T.astype(BF16)
     load_rhs.wait()
+
+    wait_all(indices, all_recv, 0)
+
+    def spread(g, extent):
+        values = indices[pl.ds(g * group, group)]
+        values = jnp.broadcast_to(values, (group, primals, lanes))
+        diagonal = lax.broadcasted_iota(jnp.int32, values.shape, 1) == lax.broadcasted_iota(
+            jnp.int32, values.shape, 2
+        )
+        named = jnp.sum(jnp.where(diagonal, values, 0.0), axis=2, keepdims=True)
+        named = named.astype(jnp.int32)
+        return jnp.broadcast_to(named, (group, primals, extent))
+
+    def choose(g, carry):
+        named = spread(g, height) - row * height
+        hit = lax.broadcasted_iota(jnp.int32, named.shape, 2) == named
+        hit = jnp.where(hit, 1.0, 0.0).astype(F32).reshape(group * primals, height).astype(BF16)
+        picked = jnp.dot(hit, coarse_ref[...], preferred_element_type=F32)
+        chosen[pl.ds(g * group, group)] = picked.reshape(group, primals, width).astype(BF16)
+        return carry
+
+    lax.fori_loop(0, count // group, choose, 0)
+    arrived[me] = chosen[me]
+
+    each_other(
+        lambda target: pltpu.make_async_remote_copy(
+            src_ref=chosen.at[target],
+            dst_ref=arrived.at[me],
+            send_sem=all_send.at[2],
+            recv_sem=all_recv.at[2],
+            device_id=place(target),
+            device_id_type=MESH,
+        ).start()
+    )
 
     load = jnp.zeros((primals, rhs_ref.shape[1]), F32)
     for f in (2, 3, 0, 1):
@@ -155,71 +189,41 @@
     loads[me] = load.astype(BF16)
     broadcast(loads, 1)
 
-    wait_all(indices, all_recv, 0)
-
-    def spread(g, extent):
-        values = indices[pl.ds(g * group, group)]
-        values = jnp.broadcast_to(values, (group, primals, lanes))
-        diagonal = lax.broadcasted_iota(jnp.int32, values.shape, 1) == lax.broadcasted_iota(
-            jnp.int32, values.shape, 2
-        )
-        named = jnp.sum(jnp.where(diagonal, values, 0.0), axis=2, keepdims=True)
-        named = named.astype(jnp.int32)
-        return jnp.broadcast_to(named, (group, primals, extent))
-
-    def choose(g, carry):
-        named = spread(g, height) - row * height
-        hit = lax.broadcasted_iota(jnp.int32, named.shape, 2) == named
-        hit = jnp.where(hit, 1.0, 0.0).astype(F32).reshape(group * primals, height).astype(BF16)
-        picked = jnp.dot(hit, coarse_ref[...], preferred_element_type=F32)
-        chosen[pl.ds(g * group, group)] = picked.reshape(group, primals, width).astype(BF16)
-        return carry
-
-    lax.fori_loop(0, count // group, choose, 0)
-    arrived[me] = chosen[me]
-
-    each_other(
-        lambda target: pltpu.make_async_remote_copy(
-            src_ref=chosen.at[target],
-            dst_ref=arrived.at[me],
-            send_sem=all_send.at[2],
-            recv_sem=all_recv.at[2],
-            device_id=place(target),
-            device_id_type=MESH,
-        ).start()
-    )
-
     load_inverse.wait()
     for f in range(4):
         block = pl.ds(f * face, face)
         z_ref[block, :] = jnp.dot(inverse_ref[block, :], weighted[...], preferred_element_type=F32)
 
-    wait_all(loads, all_recv, 1)
-    vector[...] = jnp.zeros_like(vector)
-
-    def gather(g, carry):
-        part = loads[pl.ds(g * group, group)].astype(F32).reshape(group * primals, loads.shape[2])
-        part = part.astype(BF16)
+    wait_all(arrived, all_recv, 2)
+    for j in range(cols):
+        def add(i, total):
+            return total + arrived[i * cols + j].astype(F32)
+
+        rows_ref[j] = lax.fori_loop(0, subs, add, jnp.zeros((primals, width), F32), unroll=subs <= 8)
+
+    def arrange(g, carry):
+        total = jnp.zeros((primals, group * primals), F32)
         for j in range(cols):
             named = spread(g, width) - j * width
             hit = lax.broadcasted_iota(jnp.int32, named.shape, 2) == named
             hit = jnp.where(hit, 1.0, 0.0).astype(F32).reshape(group * primals, width).astype(BF16)
-            vector[j] += lax.dot_general(
-                hit, part, (((0,), (0,)), ((), ())), preferred_element_type=F32
+            total += lax.dot_general(
+                rows_ref[j].astype(BF16), hit, (((1,), (1,)), ((), ())), preferred_element_type=F32
             )
+        columns[g] = total
         return carry
 
-    lax.fori_loop(0, count // group, gather, 0)
-
-    wait_all(arrived, all_recv, 2)
-    taken = jnp.zeros((primals, loads.shape[2]), F32)
-    for j in range(cols):
-        def add(i, total):
-            return total + arrived[i * cols + j].astype(F32)
-
-        rows = lax.fori_loop(0, subs, add, jnp.zeros((primals, width), F32), unroll=subs <= 8)
-        taken += jnp.dot(rows.astype(BF16), vector[j].astype(BF16), preferred_element_type=F32)
-    taken = taken.astype(BF16)
+    lax.fori_loop(0, count // group, arrange, 0)
+
+    wait_all(loads, all_recv, 1)
+
+    def solve(g, total):
+        part = loads[pl.ds(g * group, group)].astype(F32).reshape(group * primals, loads.shape[2])
+        return total + jnp.dot(columns[g].astype(BF16), part.astype(BF16), preferred_element_type=F32)
+
+    taken = lax.fori_loop(
+        0, count // group, solve, jnp.zeros((primals, loads.shape[2]), F32)
+    ).astype(BF16)
 
     z_copies = halo_copies(lambda g: z_half.at[pl.ds(g * face, face)], halo_z, z_send, z_recv)
     for f in range(4):
@@ -285,7 +289,8 @@
         near = pl.BlockSpec(memory_space=pltpu.VMEM)
         fixed = 4 * size * size + 8 * face * face + 22 * size * cases
         slots = count * (4 * 8 * lanes + 8 * primals * width + 4 * primals * cases + 4 * 8 * cases)
-        blocks = 4 * cols * width * cases
+        blocks = 4 * primals * (count * primals + cols * width)
+        group = math.gcd(count, 32)
         limit = min(fixed + slots + blocks + 4 * 1024 * 1024, 63 * 1024 * 1024)
         first, alpha = pl.pallas_call(
             functools.partial(kernel, subs, cols),
@@ -314,7 +319,8 @@
                 pltpu.VMEM((count, 1, lanes), F32),
                 pltpu.VMEM((count, primals, width), BF16),
                 pltpu.VMEM((count, primals, width), BF16),
-                pltpu.VMEM((cols, width, cases), F32),
+                pltpu.VMEM((count // group, primals, group * primals), F32),
+                pltpu.VMEM((cols, primals, width), F32),
                 pltpu.VMEM((count, primals, cases), BF16),
                 pltpu.VMEM((count, 2, cases), F32),
                 pltpu.SemaphoreType.DMA((8,)),

time: 29.7 us -> 29 us (0.976)
  Pallas kernels: 28.8 us -> 28.1 us
    pallas_call x1, Pallas kernels: 28.8 us -> 28.1 us  [step(): pl.pallas_call(functools.partial(kernel, subs, cols), out_shape=(jax.Shap...]
where the time goes in v4:
time: 29 us; the launch traced here: 28.8 us
  Pallas kernels  28.1 us (97%)
  other arithmetic  0.73 us (3%)
    pallas_call x1, Pallas kernels, step(): pl.pallas_call(functools.partial(kernel, subs, cols), out_shape=(jax.Shap...  28.1 us
    broadcast_in_dim x1, other arithmetic, step(): return (alpha * first).astype(BF16)[None]  0.73 us

profile of v4, /device:TPU:0, one launch (start us, length us, event | category | flops | bytes accessed | tf_op | source)
XLA Modules:
  0.0 28.8 jit_solution(9522762641817895220)
XLA Ops:
  0.0 28.1 %shard_map.73 = (f32[1024,128]{1,0:T(8,128)S(1)}, f32[1,128]{1,0:T(1,128)S(1)}) custom-call(bf16[1,1024,128]{2,1,0:T(8,128)(2,1)} %rhs_hbm.1, bf16[1,1024,1024]{2,1,0:T(8,128)(2,1)} %schur_hbm.1, bf16[1,1024,1024]{2,1,0:T(8,128)(2,1)} %inverse_hbm.1, bf16[1,8,1024]{2,1,0:T(8,128)(2,1)} %basis_hbm.1, bf16[32,64]{1,0:T(8,128)(2,1)} %coarse_hbm.1, ...), custom_call_target="tpu_custom_call" | custom-call | tf_op jit(solution)/shard_map/pallas_call | solution.py:295
  28.1 0.7 %fusion = bf16[1,1024,128]{2,1,0:T(8,128)(2,1)} fusion(f32[1024,128]{1,0:T(8,128)S(1)} %get-tuple-element.8, f32[128]{0:T(128)S(1)} %bitcast.3), kind=kLoop, calls=%fused_computation.1 | loop fusion | flops 262144 | bytes 786944 | tf_op jit(solution)/shard_map/broadcast_in_dim | solution.py:338
